TPU v7x, 32 devices: a whole 2x2x4 slice. The times are simulated.
32 devices in a mesh: league: 4 (over x, core), env: 8 (over z, y).
Axes of the slice: x: 2, y: 2, z: 4, core: 2. Of those that a mesh axis runs over, the one named last changes fastest.
Arguments:
- obs_own: bfloat16 [4, 2, 128, 16, 2048], P('league', None, 'env'), may hold values from -6 to 6
- obs_opp: bfloat16 [4, 2, 128, 16, 2048], P('league', None, 'env'), may hold values from -6 to 6
- actions: int32 [4, 2, 2, 128, 16], P('league', None, None, 'env'), may hold values from 0 to 255
- opponent_picks: int32 [4, 2], P('league'), may hold values from 0 to 3
- policy_weight: bfloat16 [4, 2048, 2048], P('league', 'env'), may hold values from -0.125 to 0.125
- policy_gain: bfloat16 [4, 2048], P('league'), may hold values from 0.25 to 1.75
- action_table: bfloat16 [256, 2048], replicated, may hold values from -6 to 6
- value_gain: bfloat16 [2048], replicated, may hold values from 0.25 to 1.75
- value_up: bfloat16 [2048, 1024], replicated, may hold values from -0.125 to 0.125
- value_out: bfloat16 [1024], replicated, may hold values from -0.1875 to 0.1875
Outputs:
- learner_rows: bfloat16 [4, 2, 16, 2048, 128], P('league', None, None, 'env')
- values: float32 [4, 2, 128, 16], P('league', None, 'env')
All inputs are finite; a program needn't handle non-finite values.
Results may differ from a plain program's by a relative error of at most 0.0054.
Values may be sent and summed in bfloat16 or wider, within the bound.
A program may use at most 128 MiB of HBM per device.

v0:
```python
import jax
import jax.numpy as jnp
from jax import lax
from jax.sharding import PartitionSpec as P


def rms_norm(inputs, gain):
    scale = lax.rsqrt(jnp.mean(inputs * inputs, axis=-1, keepdims=True) + 1e-05)
    return inputs * scale * gain.astype(jnp.float32)


def local(
    obs_own,
    obs_opp,
    actions,
    opponent_picks,
    policy_weight,
    policy_gain,
    action_table,
    value_gain,
    value_up,
    value_out,
):
    round_count = obs_own.shape[1]
    env_count = obs_own.shape[2]
    step_count = obs_own.shape[3]
    model_width = obs_own.shape[4]
    row_count = env_count * step_count
    weight_shard = policy_weight[0]
    own_gain = policy_gain[0]
    group_count = lax.axis_size("league")
    my_group = lax.axis_index("league")
    own_inputs = obs_own[0].reshape(round_count * row_count, model_width).astype(jnp.float32)
    own_normed = rms_norm(own_inputs, own_gain).astype(jnp.bfloat16)
    own_whole = lax.all_gather(weight_shard, "env", axis=0, tiled=True)
    own_state = own_inputs + jnp.dot(own_normed, own_whole, preferred_element_type=jnp.float32)
    every_pick = lax.all_gather(opponent_picks, "league", axis=0, tiled=True)
    action_range = jnp.arange(action_table.shape[0], dtype=jnp.int32)
    traj_list = []
    value_list = []
    for round_index in range(round_count):
        opp_raw = obs_opp[0, round_index].reshape(row_count, model_width)
        opp_inputs = opp_raw.astype(jnp.float32)
        all_rows = lax.all_gather(opp_raw, "league", axis=0, tiled=True)
        all_normed = rms_norm(all_rows.astype(jnp.float32), own_gain).astype(jnp.bfloat16)
        products = jnp.dot(all_normed, own_whole, preferred_element_type=jnp.float32)
        served = (every_pick[:, round_index] == my_group).astype(jnp.float32)
        products = (
            products.reshape(group_count, row_count, model_width) * served[:, None, None]
        ).reshape(group_count * row_count, model_width)
        opp_state = opp_inputs + lax.psum_scatter(
            products, "league", scatter_dimension=0, tiled=True
        )
        own_ids = actions[0, 0, round_index].reshape(row_count)
        opp_ids = actions[0, 1, round_index].reshape(row_count)
        onehot = (own_ids[:, None] == action_range[None, :]).astype(jnp.bfloat16) + (
            opp_ids[:, None] == action_range[None, :]
        ).astype(jnp.bfloat16)
        action_sum = jnp.dot(onehot, action_table, preferred_element_type=jnp.float32)
        round_state = lax.dynamic_slice_in_dim(own_state, round_index * row_count, row_count, 0)
        joint_sum = round_state + opp_state + action_sum
        joint_row = rms_norm(joint_sum, value_gain).astype(jnp.bfloat16)
        value_hidden = jax.nn.silu(
            jnp.dot(joint_row, value_up, preferred_element_type=jnp.float32)
        ).astype(jnp.bfloat16)
        value_est = jnp.dot(value_hidden, value_out, preferred_element_type=jnp.float32)
        value_list.append(value_est.reshape(env_count, step_count))
        time_block = joint_row.reshape(env_count, step_count, model_width).transpose(1, 2, 0)
        traj_list.append(lax.all_to_all(time_block, "env", split_axis=1, concat_axis=2, tiled=True))
    learner_rows = jnp.stack(traj_list)
    values = jnp.stack(value_list)
    return (learner_rows[None], values[None])


def solution(mesh):
    in_specs = (
        P("league", None, "env", None, None),
        P("league", None, "env", None, None),
        P("league", None, None, "env", None),
        P("league", None),
        P("league", "env", None),
        P("league", None),
        P(),
        P(),
        P(),
        P(),
    )
    out_specs = (P("league", None, None, "env", None), P("league", None, "env", None))
    return jax.shard_map(local, mesh=mesh, in_specs=in_specs, out_specs=out_specs, check_vma=False)
```

profile of v0, /device:TPU:0, one launch (start us, length us, event | category | flops | bytes accessed | tf_op | source)
XLA Modules:
  0.0 480.6 jit_solution(18280044370628031255)
XLA Ops:
  7.2 3.2 fusion.49
  12.0 6.0 %all-gather.1 = s32[4,1,2]{2,1,0:T(1,128)S(1)} all-gather(s32[1,1,2]{2,1,0:T(1,128)S(1)} %bitcast.98), channel_id=1, replica_groups=mesh['league'=4,'env'=8] {'league'}, dimensions={0}, use_global_device_ids=true | all-gather | bytes 40 | tf_op jit(solution)/shard_map/all_gather | solution.py:37
  18.2 29.6 %all-gather.6.cloned.1.call-done = bf16[1024,2048]{1,0:T(8,128)(2,1)} async-done(((bf16[256,2048]{1,0:T(8,128)(2,1)}), bf16[1024,2048]{1,0:T(8,128)(2,1)}) %all-gather.6.cloned.1.call-update) | async-done | bytes 4194320 | tf_op jit(solution)/shard_map/all_gather | solution.py:44
  47.8 3.1 fusion
  50.9 124.0 %all-gather.10.cloned.1.call-done = bf16[1,2048,2048]{2,1,0:T(8,128)(2,1)} async-done(((bf16[1,256,2048]{2,1,0:T(8,128)(2,1)}), bf16[1,2048,2048]{2,1,0:T(8,128)(2,1)}) %all-gather.10.cloned.1.call-update) | async-done | bytes 8388624 | tf_op jit(solution)/shard_map/all_gather | solution.py:35
  174.9 14.5 %fusion.12 = f32[1024,2048]{1,0:T(8,128)} fusion(bf16[1,2048,2048]{2,1,0:T(8,128)(2,1)} %all-gather.10.cloned.1.call-done, bf16[1024,2048]{1,0:T(8,128)(2,1)} %all-gather.6.cloned.1.call-done, f32[1024]{0:T(1024)S(1)} %bitcast.94, f32[2048]{0:T(1024)S(1)} %bitcast.90, f32[1024]{0:T(1024)S(1)} %add_rsqrt_fusion.2), kind=kOutput, calls=%fused_computation.16 | convolution fusion | flops 8600420352 | bytes 20987904 | tf_op jit(solution)/shard_map/dot_general | solution.py:46
  189.7 19.5 %all-gather.8.cloned.1.call-done = bf16[1024,2048]{1,0:T(8,128)(2,1)} async-done(((bf16[256,2048]{1,0:T(8,128)(2,1)}), bf16[1024,2048]{1,0:T(8,128)(2,1)}) %all-gather.8.cloned.1.call-update) | async-done | bytes 4194320 | tf_op jit(solution)/shard_map/all_gather | solution.py:44
  209.2 3.2 fusion.3
  212.6 13.6 %fusion.15 = f32[1024,2048]{1,0:T(8,128)} fusion(bf16[1,2048,2048]{2,1,0:T(8,128)(2,1)} %all-gather.10.cloned.1.call-done, bf16[1024,2048]{1,0:T(8,128)(2,1)S(1)} %copy-done.6, f32[1024]{0:T(1024)S(1)} %bitcast.95, f32[1024]{0:T(1024)S(1)} %add_rsqrt_fusion.1, f32[2048]{0:T(1024)S(1)} %bitcast.91), kind=kOutput, calls=%fused_computation.17 | convolution fusion | flops 8600420352 | bytes 20987904 | tf_op jit(solution)/shard_map/dot_general | solution.py:46
  227.1 0.8 copy-done.4
  229.2 1.0 copy-done.5
  230.2 9.6 %bitcast_add_fusion = f32[512,2048]{1,0:T(8,128)} fusion(bf16[1,2,16,16,2048]{4,3,2,1,0:T(8,128)(2,1)S(1)} %copy-done.5, bf16[512,2048]{1,0:T(8,128)(2,1)S(1)} %fusion.22, bf16[1,2048,2048]{2,1,0:T(8,128)(2,1)} %all-gather.10.cloned.1.call-done), kind=kOutput, calls=%fused_computation.18 | convolution fusion | flops 4297064448 | bytes 16777216 | tf_op jit(solution)/shard_map/dot_general | solution.py:36
  239.9 43.5 %reduce-scatter.3.cloned.1.call-done = f32[256,2048]{1,0:T(8,128)} async-done(((f32[1024,2048]{1,0:T(8,128)}), f32[256,2048]{1,0:T(8,128)}) %reduce-scatter.3.cloned.1.call-update) | async-done | bytes 2097168 | tf_op jit(solution)/shard_map/reduce_scatter | solution.py:51
  283.4 4.2 multiply_reduce_fusion.1
  287.6 70.1 %reduce-scatter.5.cloned.1.call-done = f32[256,2048]{1,0:T(8,128)} async-done(((f32[1024,2048]{1,0:T(8,128)}), f32[256,2048]{1,0:T(8,128)}) %reduce-scatter.5.cloned.1.call-update) | async-done | bytes 2097168 | tf_op jit(solution)/shard_map/reduce_scatter | solution.py:51
  357.7 3.1 multiply_reduce_fusion
  361.3 8.8 %copy.27 = bf16[16,16,2048]{0,1,2:T(8,128)(2,1)} copy(bf16[16,16,2048]{2,1,0:T(8,128)(2,1)S(1)} %bitcast.87) | data formatting | bytes 2097152 | tf_op jit(solution)/shard_map/reshape | solution.py:68
  370.1 7.5 %bitcast_bitcast_fusion = bf16[2048,16,16]{2,1,0:T(8,128)(2,1)} fusion(bf16[16,16,2048]{0,1,2:T(8,128)(2,1)} %copy.27), kind=kLoop, calls=%fused_computation.71 | loop fusion | bytes 2097152
  377.6 11.2 %reshape.107 = bf16[8,2,32768]{2,1,0:T(2,128)(2,1)} reshape(bf16[2048,16,16]{2,1,0:T(8,128)(2,1)} %bitcast_bitcast_fusion) | data formatting | bytes 2097152
  388.8 5.5 %all-to-all-start.1 = ((bf16[8,2,32768]{2,1,0:T(2,128)(2,1)}), bf16[8,2,32768]{2,1,0:T(2,128)(2,1)S(1)}, u32[]{:S(2)}, u32[]{:S(2)}) async-start(bf16[8,2,32768]{2,1,0:T(2,128)(2,1)} %reshape.107), calls=%async_computation.3 | async-start | bytes 2097152 | tf_op jit(solution)/shard_map/all_to_all | solution.py:69
  394.3 8.8 %copy.24 = bf16[16,16,2048]{0,1,2:T(8,128)(2,1)} copy(bf16[16,16,2048]{2,1,0:T(8,128)(2,1)S(1)} %bitcast.86) | data formatting | bytes 2097152 | tf_op jit(solution)/shard_map/reshape | solution.py:68
  403.1 7.5 %bitcast_bitcast_fusion.1 = bf16[2048,16,16]{2,1,0:T(8,128)(2,1)} fusion(bf16[16,16,2048]{0,1,2:T(8,128)(2,1)} %copy.24), kind=kLoop, calls=%fused_computation.72 | loop fusion | bytes 2097152
  410.6 11.2 %reshape.109 = bf16[8,2,32768]{2,1,0:T(2,128)(2,1)} reshape(bf16[2048,16,16]{2,1,0:T(8,128)(2,1)} %bitcast_bitcast_fusion.1) | data formatting | bytes 2097152
  421.8 6.0 %all-to-all-start = ((bf16[8,2,32768]{2,1,0:T(2,128)(2,1)}), bf16[8,2,32768]{2,1,0:T(2,128)(2,1)S(1)}, u32[]{:S(2)}, u32[]{:S(2)}) async-start(bf16[8,2,32768]{2,1,0:T(2,128)(2,1)} %reshape.109), calls=%async_computation.1 | async-start | bytes 2097152 | tf_op jit(solution)/shard_map/all_to_all | solution.py:69
  427.9 3.9 fusion.30
  431.9 4.0 fusion.29
  436.6 7.5 %reshape.108 = bf16[2048,16,16]{2,1,0:T(8,128)(2,1)} reshape(bf16[8,2,32768]{2,1,0:T(2,128)(2,1)S(1)} %all-to-all-done.1) | data formatting | bytes 2097152
  444.1 9.1 %copy.29 = bf16[16,256,8,16]{1,3,2,0:T(8,128)(2,1)} copy(bf16[16,256,8,16]{3,0,1,2:T(8,128)(2,1)} %bitcast.80) | data formatting | bytes 2097152 | tf_op jit(solution)/shard_map/all_to_all | solution.py:69
  453.3 7.5 %reshape.110 = bf16[2048,16,16]{2,1,0:T(8,128)(2,1)} reshape(bf16[8,2,32768]{2,1,0:T(2,128)(2,1)S(1)} %all-to-all-done) | data formatting | bytes 2097152
  460.8 9.1 %copy.26 = bf16[16,256,8,16]{1,3,2,0:T(8,128)(2,1)} copy(bf16[16,256,8,16]{3,0,1,2:T(8,128)(2,1)} %bitcast.81) | data formatting | bytes 2097152 | tf_op jit(solution)/shard_map/all_to_all | solution.py:69
  469.9 1.7 maximum_bitcast_fusion
  471.7 2.4 copy.30
  (63 shorter events, 5.8 us)
Async XLA Ops:
  7.2 276.2 %copy-start = (bf16[256,2048]{1,0:T(8,128)(2,1)S(1)}, bf16[256,2048]{1,0:T(8,128)(2,1)}, u32[]{:S(2)}) copy-start(bf16[256,2048]{1,0:T(8,128)(2,1)} %param.16) | copy-start | bytes 3145732
  7.2 4.8 %copy-start.13 = (s32[1,2]{1,0:T(1,128)S(1)}, s32[1,2]{1,0:T(1,128)}, u32[]{:S(2)}) copy-start(s32[1,2]{1,0:T(1,128)} %param.13) | copy-start | bytes 28
  7.2 11.0 %copy-start.10 = (bf16[1,2048]{1,0:T(2,128)(2,1)S(1)}, bf16[1,2048]{1,0:T(2,128)(2,1)}, u32[]{:S(2)}) copy-start(bf16[1,2048]{1,0:T(2,128)(2,1)} %param.15) | copy-start | bytes 12292
  7.2 40.6 %all-gather.6.cloned.1.call-start = ((), (), s32[]{:S(2)}) async-start(), calls=%async_computation.4 | async-start | bytes 5242880 | tf_op jit(solution)/shard_map/all_gather | solution.py:44
  10.5 164.4 %all-gather.10.cloned.1.call-start = ((), (), s32[]{:S(2)}) async-start(), calls=%async_computation.8 | async-start | bytes 9437184 | tf_op jit(solution)/shard_map/all_gather | solution.py:35
  11.2 197.9 %all-gather.8.cloned.1.call-start = ((), (), s32[]{:S(2)}) async-start(), calls=%async_computation.6 | async-start | bytes 5242880 | tf_op jit(solution)/shard_map/all_gather | solution.py:44
  12.0 271.4 %reduce-scatter.3.cloned.1.call-start = ((), (), s32[]{:S(2)}) async-start(), calls=%async_computation.5 | async-start | bytes 10485760 | tf_op jit(solution)/shard_map/reduce_scatter | solution.py:51
  189.5 168.2 %reduce-scatter.5.cloned.1.call-start = ((), (), s32[]{:S(2)}) async-start(), calls=%async_computation.7 | async-start | bytes 10485760 | tf_op jit(solution)/shard_map/reduce_scatter | solution.py:51
  209.2 3.4 copy-start.6
  226.2 0.8 copy-start.9
  226.2 1.7 copy-start.4
  226.2 2.3 copy-start.11
  228.6 1.6 copy-start.5
  230.2 53.1 %copy-start.2 = (bf16[1,1,16,16,2048]{4,3,2,1,0:T(8,128)(2,1)S(1)}, bf16[1,1,16,16,2048]{4,3,2,1,0:T(8,128)(2,1)}, u32[]{:S(2)}) copy-start(bf16[1,1,16,16,2048]{4,3,2,1,0:T(8,128)(2,1)} %get-tuple-element.8) | copy-start | bytes 3145732
  239.9 117.8 %copy-start.1 = (bf16[1,1,16,16,2048]{4,3,2,1,0:T(8,128)(2,1)S(1)}, bf16[1,1,16,16,2048]{4,3,2,1,0:T(8,128)(2,1)}, u32[]{:S(2)}) copy-start(bf16[1,1,16,16,2048]{4,3,2,1,0:T(8,128)(2,1)} %get-tuple-element.9) | copy-start | bytes 3145732
  357.7 3.1 copy-start.3
  361.2 8.8 %copy-start.8 = (bf16[256,2048]{1,0:T(8,128)(2,1)}, bf16[256,2048]{1,0:T(8,128)(2,1)S(1)}, u32[]{:S(2)}) copy-start(bf16[256,2048]{1,0:T(8,128)(2,1)S(1)} %get-tuple-element.15) | copy-start | bytes 3145732
  361.3 33.1 %copy-start.7 = (bf16[256,2048]{1,0:T(8,128)(2,1)}, bf16[256,2048]{1,0:T(8,128)(2,1)S(1)}, u32[]{:S(2)}) copy-start(bf16[256,2048]{1,0:T(8,128)(2,1)S(1)} %get-tuple-element.14) | copy-start | bytes 3145732
  388.8 33.0 %all-to-all-start.1 = ((bf16[8,2,32768]{2,1,0:T(2,128)(2,1)}), bf16[8,2,32768]{2,1,0:T(2,128)(2,1)S(1)}, u32[]{:S(2)}, u32[]{:S(2)}) async-start(bf16[8,2,32768]{2,1,0:T(2,128)(2,1)} %reshape.107), calls=%async_computation.3 | async-start | bytes 2097152 | tf_op jit(solution)/shard_map/all_to_all | solution.py:69
  410.6 17.2 %copy-start.12 = (bf16[1024]{0:T(1024)(128)(2,1)S(1)}, bf16[1024]{0:T(1024)(128)(2,1)}, u32[]{:S(2)}) copy-start(bf16[1024]{0:T(1024)(128)(2,1)} %param.19) | copy-start | bytes 6148
  421.8 31.4 %all-to-all-start = ((bf16[8,2,32768]{2,1,0:T(2,128)(2,1)}), bf16[8,2,32768]{2,1,0:T(2,128)(2,1)S(1)}, u32[]{:S(2)}, u32[]{:S(2)}) async-start(bf16[8,2,32768]{2,1,0:T(2,128)(2,1)} %reshape.109), calls=%async_computation.1 | async-start | bytes 2097152 | tf_op jit(solution)/shard_map/all_to_all | solution.py:69
Sparse Core Ops, SparseCore 0:
  10.6 37.1 all-gather.5
  49.9 124.9 all-gather.9
  176.5 32.6 all-gather.7
  211.6 71.7 reduce-scatter.2
  286.0 71.6 reduce-scatter.4
where the time goes:
time: 482 us; the launch traced here: 481 us
  waiting for transfers between devices  288 us (60%)
  local copies, waits for them, and re-layouts  97.5 us (20%)
  matrix products  52.9 us (11%)
  between operations  13.9 us (3%)
  starting transfers between devices  11.9 us (2%)
  other arithmetic  10.2 us (2%)
  blocking collectives  5.95 us (1%)
    all_gather x1, waiting for transfers between devices, local(): own_whole = lax.all_gather(weight_shard, 'env', axis=0, tiled=True)  124 us
    reduce_scatter x2, waiting for transfers between devices, local(): lax.psum_scatter(products, 'league', scatter_dimension=0, tiled=True)  114 us
    unnamed x39, local copies, waits for them, and re-layouts  57.8 us
    all_gather x2, waiting for transfers between devices, local(): all_rows = lax.all_gather(opp_raw, 'league', axis=0, tiled=True)  49.1 us
    dot_general x2, matrix products, local(): jnp.dot(all_normed, own_whole, preferred_element_type=jnp.float32)  28.1 us
    all_to_all x2, local copies, waits for them, and re-layouts, local(): lax.all_to_all(time_block, 'env', split_axis=1, concat_axis=2, tiled=True)  18.2 us
    reshape x2, local copies, waits for them, and re-layouts, local(): joint_row.reshape(env_count, step_count, model_width).transpose(1, 2, 0)  17.6 us
    all_to_all x2, starting transfers between devices, local(): lax.all_to_all(time_block, 'env', split_axis=1, concat_axis=2, tiled=True)  11.5 us
  transfers between devices with their start and end apart: 7, of which 5 were waited for; matrix products, arithmetic and copies ran while one was open for 21% of the time, Pallas kernels for 0%

commit v1 on v0

--- a/solution.py
+++ b/solution.py
@@ -66,7 +66,14 @@
         value_est = jnp.dot(value_hidden, value_out, preferred_element_type=jnp.float32)
         value_list.append(value_est.reshape(env_count, step_count))
         time_block = joint_row.reshape(env_count, step_count, model_width).transpose(1, 2, 0)
-        traj_list.append(lax.all_to_all(time_block, "env", split_axis=1, concat_axis=2, tiled=True))
+        traj_list.append(
+            jnp.concatenate(
+                lax.all_to_all(
+                    jnp.stack(jnp.split(time_block, lax.axis_size("env"), axis=1)), "env", 0, 0
+                ),
+                axis=2,
+            )
+        )
     learner_rows = jnp.stack(traj_list)
     values = jnp.stack(value_list)
     return (learner_rows[None], values[None])

time: 482 us -> 440 us (0.913)
  local copies, waits for them, and re-layouts: 97.5 us -> 19 us
  waiting for transfers between devices: 288 us -> 328 us
    unnamed x39 -> x49, local copies, waits for them, and re-layouts: 57.8 us -> 12.1 us
    all_to_all x2, waiting for transfers between devices: 0.04 us -> 39.9 us  [local(): lax.all_to_all(jnp.stack(jnp.split(time_block, lax.axis_size('env'), axis...]
    all_to_all x2, local copies, waits for them, and re-layouts: 18.2 us -> 1.19 us  [local(): lax.all_to_all(jnp.stack(jnp.split(time_block, lax.axis_size('env'), axis...]
    reshape x2, local copies, waits for them, and re-layouts: 17.6 us -> 1.16 us  [local(): joint_row.reshape(env_count, step_count, model_width).transpose(1, 2, 0)]
  transfers between devices with their start and end apart: 7 -> 7, of which waited for: 5 -> 7; matrix products, arithmetic and copies ran while one was open for 21% -> 14% of each run, Pallas kernels for 0% -> 0%
where the time goes in v1:
time: 440 us
  waiting for transfers between devices  328 us (75%)
  matrix products  53 us (12%)
  local copies, waits for them, and re-layouts  19 us (4%)
  between operations  14 us (3%)
  other arithmetic  9.89 us (2%)
  starting transfers between devices  9.8 us (2%)
  blocking collectives  5.95 us (1%)
    all_gather x1, waiting for transfers between devices, local(): own_whole = lax.all_gather(weight_shard, 'env', axis=0, tiled=True)  124 us
    reduce_scatter x2, waiting for transfers between devices, local(): lax.psum_scatter(products, 'league', scatter_dimension=0, tiled=True)  114 us
    all_gather x2, waiting for transfers between devices, local(): all_rows = lax.all_gather(opp_raw, 'league', axis=0, tiled=True)  49 us
    all_to_all x2, waiting for transfers between devices, local(): lax.all_to_all(jnp.stack(jnp.split(time_block, lax.axis_size('env'), axis...  39.9 us
    dot_general x2, matrix products, local(): jnp.dot(all_normed, own_whole, preferred_element_type=jnp.float32)  28.2 us
    unnamed x49, local copies, waits for them, and re-layouts  12.1 us
    dot_general x1, matrix products, local(): jnp.dot(own_normed, own_whole, preferred_element_type=jnp.float32)  9.62 us
    all_to_all x2, starting transfers between devices, local(): lax.all_to_all(jnp.stack(jnp.split(time_block, lax.axis_size('env'), axis...  9.42 us
  transfers between devices with their start and end apart: 7, of which 7 were waited for; matrix products, arithmetic and copies ran while one was open for 14% of the time, Pallas kernels for 0%

profile of v1, /device:TPU:0, one launch (start us, length us, event | category | flops | bytes accessed | tf_op | source)
XLA Modules:
  0.0 439.7 jit_solution(1887873405277306328)
XLA Ops:
  7.2 3.2 fusion.65
  10.5 0.7 all-gather.10.cloned.1.call-update
  11.3 0.7 all-gather.8.cloned.1.call-update
  12.0 6.0 %all-gather.1 = s32[4,1,2]{2,1,0:T(1,128)S(1)} all-gather(s32[1,1,2]{2,1,0:T(1,128)S(1)} %bitcast.168), channel_id=1, replica_groups=mesh['league'=4,'env'=8] {'league'}, dimensions={0}, use_global_device_ids=true | all-gather | bytes 40 | tf_op jit(solution)/shard_map/all_gather | solution.py:37
  18.2 29.6 %all-gather.6.cloned.1.call-done = bf16[1024,2048]{1,0:T(8,128)(2,1)} async-done(((bf16[256,2048]{1,0:T(8,128)(2,1)}), bf16[1024,2048]{1,0:T(8,128)(2,1)}) %all-gather.6.cloned.1.call-update) | async-done | bytes 4194320 | tf_op jit(solution)/shard_map/all_gather | solution.py:44
  47.8 3.1 fusion
  50.9 124.0 %all-gather.10.cloned.1.call-done = bf16[1,2048,2048]{2,1,0:T(8,128)(2,1)} async-done(((bf16[1,256,2048]{2,1,0:T(8,128)(2,1)}), bf16[1,2048,2048]{2,1,0:T(8,128)(2,1)}) %all-gather.10.cloned.1.call-update) | async-done | bytes 8388624 | tf_op jit(solution)/shard_map/all_gather | solution.py:35
  174.9 14.6 %fusion.12 = f32[1024,2048]{1,0:T(8,128)} fusion(bf16[1,2048,2048]{2,1,0:T(8,128)(2,1)} %all-gather.10.cloned.1.call-done, bf16[1024,2048]{1,0:T(8,128)(2,1)} %all-gather.6.cloned.1.call-done, f32[1024]{0:T(1024)S(1)} %bitcast.164, f32[2048]{0:T(1024)S(1)} %bitcast.160, f32[1024]{0:T(1024)S(1)} %add_rsqrt_fusion.2), kind=kOutput, calls=%fused_computation.16 | convolution fusion | flops 8600420352 | bytes 20987904 | tf_op jit(solution)/shard_map/dot_general | solution.py:46
  189.8 19.4 %all-gather.8.cloned.1.call-done = bf16[1024,2048]{1,0:T(8,128)(2,1)} async-done(((bf16[256,2048]{1,0:T(8,128)(2,1)}), bf16[1024,2048]{1,0:T(8,128)(2,1)}) %all-gather.8.cloned.1.call-update) | async-done | bytes 4194320 | tf_op jit(solution)/shard_map/all_gather | solution.py:44
  209.2 3.2 fusion.3
  212.6 13.6 %fusion.15 = f32[1024,2048]{1,0:T(8,128)} fusion(bf16[1,2048,2048]{2,1,0:T(8,128)(2,1)} %all-gather.10.cloned.1.call-done, bf16[1024,2048]{1,0:T(8,128)(2,1)S(1)} %copy-done.6, f32[1024]{0:T(1024)S(1)} %bitcast.165, f32[1024]{0:T(1024)S(1)} %add_rsqrt_fusion.1, f32[2048]{0:T(1024)S(1)} %bitcast.161), kind=kOutput, calls=%fused_computation.17 | convolution fusion | flops 8600420352 | bytes 20987904 | tf_op jit(solution)/shard_map/dot_general | solution.py:46
  226.2 0.7 copy-done.10
  227.1 0.8 copy-done.4
  229.2 1.0 copy-done.5
  230.3 9.6 %bitcast_add_fusion = f32[512,2048]{1,0:T(8,128)} fusion(bf16[1,2,16,16,2048]{4,3,2,1,0:T(8,128)(2,1)S(1)} %copy-done.5, bf16[512,2048]{1,0:T(8,128)(2,1)S(1)} %fusion.22, bf16[1,2048,2048]{2,1,0:T(8,128)(2,1)} %all-gather.10.cloned.1.call-done), kind=kOutput, calls=%fused_computation.18 | convolution fusion | flops 4297064448 | bytes 16777216 | tf_op jit(solution)/shard_map/dot_general | solution.py:36
  239.9 43.4 %reduce-scatter.3.cloned.1.call-done = f32[256,2048]{1,0:T(8,128)} async-done(((f32[1024,2048]{1,0:T(8,128)}), f32[256,2048]{1,0:T(8,128)}) %reduce-scatter.3.cloned.1.call-update) | async-done | bytes 2097168 | tf_op jit(solution)/shard_map/reduce_scatter | solution.py:51
  283.3 4.2 multiply_reduce_fusion.1
  287.5 70.2 %reduce-scatter.5.cloned.1.call-done = f32[256,2048]{1,0:T(8,128)} async-done(((f32[1024,2048]{1,0:T(8,128)}), f32[256,2048]{1,0:T(8,128)}) %reduce-scatter.5.cloned.1.call-update) | async-done | bytes 2097168 | tf_op jit(solution)/shard_map/reduce_scatter | solution.py:51
  357.7 3.1 multiply_reduce_fusion
  361.3 1.0 copy-done.8
  362.8 0.7 fusion.48
  365.5 0.7 fusion.44
  368.2 5.6 %all-to-all-start.1 = ((bf16[8,16,256,16]{2,3,1,0:T(8,128)(2,1)}), bf16[8,16,256,16]{2,3,1,0:T(8,128)(2,1)S(1)}, u32[]{:S(2)}, u32[]{:S(2)}) async-start(bf16[8,16,256,16]{2,3,1,0:T(8,128)(2,1)} %fusion.41), calls=%async_computation.3 | async-start | bytes 2097152 | tf_op jit(solution)/shard_map/all_to_all | solution.py:71
  374.7 1.0 copy-done.9
  375.7 24.0 %all-to-all-done.1 = bf16[8,16,256,16]{2,3,1,0:T(8,128)(2,1)S(1)} async-done(((bf16[8,16,256,16]{2,3,1,0:T(8,128)(2,1)}), bf16[8,16,256,16]{2,3,1,0:T(8,128)(2,1)S(1)}, u32[]{:S(2)}, u32[]{:S(2)}) %all-to-all-start.1) | async-done | bytes 1048608 | tf_op jit(solution)/shard_map/all_to_all | solution.py:71
  399.6 3.8 all-to-all-start
  403.4 3.9 fusion.30
  407.5 4.0 fusion.29
  412.2 1.1 copy.37
  413.3 16.0 %all-to-all-done = bf16[8,16,256,16]{2,3,1,0:T(8,128)(2,1)S(1)} async-done(((bf16[8,16,256,16]{2,3,1,0:T(8,128)(2,1)}), bf16[8,16,256,16]{2,3,1,0:T(8,128)(2,1)S(1)}, u32[]{:S(2)}, u32[]{:S(2)}) %all-to-all-start) | async-done | bytes 1048608 | tf_op jit(solution)/shard_map/all_to_all | solution.py:71
  429.3 1.4 maximum_bitcast_fusion
  430.8 2.4 copy.38
  (75 shorter events, 9.1 us)
Async XLA Ops:
  7.2 276.2 %copy-start = (bf16[256,2048]{1,0:T(8,128)(2,1)S(1)}, bf16[256,2048]{1,0:T(8,128)(2,1)}, u32[]{:S(2)}) copy-start(bf16[256,2048]{1,0:T(8,128)(2,1)} %param.16) | copy-start | bytes 3145732
  7.2 4.8 %copy-start.14 = (s32[1,2]{1,0:T(1,128)S(1)}, s32[1,2]{1,0:T(1,128)}, u32[]{:S(2)}) copy-start(s32[1,2]{1,0:T(1,128)} %param.13) | copy-start | bytes 28
  7.2 11.0 %copy-start.11 = (bf16[1,2048]{1,0:T(2,128)(2,1)S(1)}, bf16[1,2048]{1,0:T(2,128)(2,1)}, u32[]{:S(2)}) copy-start(bf16[1,2048]{1,0:T(2,128)(2,1)} %param.15) | copy-start | bytes 12292
  7.2 40.6 %all-gather.6.cloned.1.call-start = ((), (), s32[]{:S(2)}) async-start(), calls=%async_computation.4 | async-start | bytes 5242880 | tf_op jit(solution)/shard_map/all_gather | solution.py:44
  10.5 164.4 %all-gather.10.cloned.1.call-start = ((), (), s32[]{:S(2)}) async-start(), calls=%async_computation.8 | async-start | bytes 9437184 | tf_op jit(solution)/shard_map/all_gather | solution.py:35
  11.2 197.9 %all-gather.8.cloned.1.call-start = ((), (), s32[]{:S(2)}) async-start(), calls=%async_computation.6 | async-start | bytes 5242880 | tf_op jit(solution)/shard_map/all_gather | solution.py:44
  12.0 271.4 %reduce-scatter.3.cloned.1.call-start = ((), (), s32[]{:S(2)}) async-start(), calls=%async_computation.5 | async-start | bytes 10485760 | tf_op jit(solution)/shard_map/reduce_scatter | solution.py:51
  189.6 168.1 %reduce-scatter.5.cloned.1.call-start = ((), (), s32[]{:S(2)}) async-start(), calls=%async_computation.7 | async-start | bytes 10485760 | tf_op jit(solution)/shard_map/reduce_scatter | solution.py:51
  209.2 3.4 copy-start.6
  226.2 0.8 copy-start.10
  226.2 1.7 copy-start.4
  226.2 2.3 copy-start.12
  228.7 1.6 copy-start.5
  230.3 53.1 %copy-start.2 = (bf16[1,1,16,16,2048]{4,3,2,1,0:T(8,128)(2,1)S(1)}, bf16[1,1,16,16,2048]{4,3,2,1,0:T(8,128)(2,1)}, u32[]{:S(2)}) copy-start(bf16[1,1,16,16,2048]{4,3,2,1,0:T(8,128)(2,1)} %get-tuple-element.6) | copy-start | bytes 3145732
  239.9 117.8 %copy-start.1 = (bf16[1,1,16,16,2048]{4,3,2,1,0:T(8,128)(2,1)S(1)}, bf16[1,1,16,16,2048]{4,3,2,1,0:T(8,128)(2,1)}, u32[]{:S(2)}) copy-start(bf16[1,1,16,16,2048]{4,3,2,1,0:T(8,128)(2,1)} %get-tuple-element.7) | copy-start | bytes 3145732
  357.7 3.1 copy-start.3
  361.3 1.0 copy-start.8
  361.3 13.2 %copy-start.7 = (bf16[256,2048]{1,0:T(8,128)(2,1)}, bf16[256,2048]{1,0:T(8,128)(2,1)S(1)}, u32[]{:S(2)}) copy-start(bf16[256,2048]{1,0:T(8,128)(2,1)S(1)} %get-tuple-element.12) | copy-start | bytes 3145732
  368.2 35.2 %copy-start.13 = (bf16[1024]{0:T(1024)(128)(2,1)S(1)}, bf16[1024]{0:T(1024)(128)(2,1)}, u32[]{:S(2)}) copy-start(bf16[1024]{0:T(1024)(128)(2,1)} %param.19) | copy-start | bytes 6148
  368.2 31.4 %all-to-all-start.1 = ((bf16[8,16,256,16]{2,3,1,0:T(8,128)(2,1)}), bf16[8,16,256,16]{2,3,1,0:T(8,128)(2,1)S(1)}, u32[]{:S(2)}, u32[]{:S(2)}) async-start(bf16[8,16,256,16]{2,3,1,0:T(8,128)(2,1)} %fusion.41), calls=%async_computation.3 | async-start | bytes 2097152 | tf_op jit(solution)/shard_map/all_to_all | solution.py:71
  374.7 1.0 copy-start.9
  399.6 29.6 %all-to-all-start = ((bf16[8,16,256,16]{2,3,1,0:T(8,128)(2,1)}), bf16[8,16,256,16]{2,3,1,0:T(8,128)(2,1)S(1)}, u32[]{:S(2)}, u32[]{:S(2)}) async-start(bf16[8,16,256,16]{2,3,1,0:T(8,128)(2,1)} %copy-done.9), calls=%async_computation.1 | async-start | bytes 2097152 | tf_op jit(solution)/shard_map/all_to_all | solution.py:71
Sparse Core Ops, SparseCore 0:
  10.6 37.1 all-gather.5
  49.9 124.9 all-gather.9
  176.5 32.6 all-gather.7
  211.6 71.6 reduce-scatter.2
  285.9 71.7 reduce-scatter.4
